TPU v7x, 512 devices: a whole 4x8x8 slice. The times are simulated.
512 devices in a mesh: layer: 32 (over x_lo, y, core), feat: 16 (over z, x_hi).
Axes of the slice: x: 4 (x_hi: 2, x_lo: 2; x = x_hi * 2 + x_lo), y: 8, z: 8, core: 2. Of those that a mesh axis runs over, the one named last changes fastest.
Arguments:
- latents: bfloat16 [2048, 16384], P('layer', 'feat'), may hold values from 0.5 to 3
- block_lists: int32 [4, 16, 64], replicated, may hold values from 0 to 127, all different within a row
- decoders: bfloat16 [2, 16384, 32768], P(None, 'feat', 'layer'), may hold values from -0.03125 to 0.03125
- targets: bfloat16 [512, 32768], P('feat', 'layer'), may hold values from -6 to 6
Outputs:
- errors: bfloat16 [512, 32768], P('feat', 'layer')
- latent_grad: float32 [2048, 16384], P('layer', 'feat')
Inputs may be any that keep to these rules, and one draw needn't show every extreme that they name: `block_lists`: each row names 64 different latent blocks, and every block is named by some row.
All inputs are finite; a program needn't handle non-finite values.
Results may differ from a plain program's by a relative error of at most 0.006.
Values may be sent and summed in bfloat16 or wider, within the bound.
No kernel may reach another device: no remote copies, remote signals or barrier semaphores. Data moves between devices by JAX's collectives and lax.ppermute only.
A program may use at most 64 MiB of HBM per device.

v0:
```python
import jax
import jax.numpy as jnp
from jax import lax
from jax.sharding import PartitionSpec as P

D = 8192
BLOCK = 128


def swapped(value, axis, bit):
    mask = 2**bit
    pairs = [(source, source ^ mask) for source in range(lax.axis_size(axis))]
    return lax.ppermute(value, axis, pairs)


def passed_along(value, axis, steps):
    count = lax.axis_size(axis)
    first, last = (max(0, -steps), min(count, count - steps))
    return lax.ppermute(value, axis, [(source, source + steps) for source in range(first, last)])


def doubled(held_rows, partner_rows, upper_half):
    return jnp.where(
        upper_half,
        jnp.concatenate([partner_rows, held_rows], 0),
        jnp.concatenate([held_rows, partner_rows], 0),
    )


def pick_half(block, upper_half, axis):
    half_rows = block.shape[axis] // 2
    lower = lax.slice_in_dim(block, 0, half_rows, axis=axis)
    higher = lax.slice_in_dim(block, half_rows, 2 * half_rows, axis=axis)
    return (jnp.where(upper_half, higher, lower), jnp.where(upper_half, lower, higher))


def local(latents, block_lists, decoders, targets):
    layer_pos = lax.axis_index("layer")
    feat_pos = lax.axis_index("feat")
    width_cols = decoders.shape[2]
    groups = D // width_cols
    width_bits = groups.bit_length() - 1
    layer_id = layer_pos // groups
    member = layer_pos % groups
    quarter, feat_cols = latents.shape
    total_rows = quarter * groups
    block_rows = total_rows // block_lists.shape[1]
    blocks_here = feat_cols // BLOCK
    lists = lax.dynamic_index_in_dim(block_lists, layer_id, 0, keepdims=False)
    wanted = feat_pos * blocks_here + jnp.arange(blocks_here, dtype=jnp.int32)
    hit = jnp.any(lists[:, :, None] == wanted[None, None, :], axis=1)
    row_hit = jnp.repeat(hit, block_rows, axis=0)
    row_hit = lax.dynamic_slice_in_dim(row_hit, member * quarter, quarter, 0)
    tile_mask = jnp.repeat(row_hit, BLOCK, axis=1)
    own_tile = jnp.where(tile_mask, latents, jnp.zeros_like(latents))
    own_all = own_tile
    for bit_pos in range(width_bits):
        upper_half = member // (1 << bit_pos) % 2 == 1
        partner_rows = swapped(own_all, "layer", bit_pos)
        own_all = doubled(own_all, partner_rows, upper_half)
    prior_all = passed_along(own_all, "layer", groups)
    summed = jnp.dot(own_all, decoders[0], preferred_element_type=jnp.float32)
    recon_rows = lax.psum_scatter(
        summed + jnp.dot(prior_all, decoders[1], preferred_element_type=jnp.float32),
        "feat",
        scatter_dimension=0,
        tiled=True,
    )
    errors_here = (recon_rows - targets.astype(jnp.float32)).astype(jnp.bfloat16)
    grad_terms = jnp.einsum(
        "tc,kfc->ktf",
        lax.all_gather(errors_here, "feat", axis=0, tiled=True),
        decoders,
        preferred_element_type=jnp.float32,
    )
    grad_pair = grad_terms
    for bit_pos in reversed(range(width_bits)):
        upper_half = member // (1 << bit_pos) % 2 == 1
        kept_part, sent_part = pick_half(grad_pair, upper_half, 1)
        grad_pair = kept_part + swapped(sent_part.astype(jnp.bfloat16), "layer", bit_pos).astype(
            sent_part.dtype
        )
    from_next = passed_along(grad_pair[1].astype(jnp.bfloat16), "layer", -groups).astype(
        jnp.float32
    )
    combined = grad_pair[0] + from_next
    latent_grad = jnp.where(tile_mask, combined, jnp.zeros_like(combined))
    return (errors_here, latent_grad)


def solution(mesh):
    placed = (P("layer", "feat"), P(), P(None, "feat", "layer"), P("feat", "layer"))
    return jax.shard_map(
        local,
        mesh=mesh,
        in_specs=placed,
        out_specs=(P("feat", "layer"), P("layer", "feat")),
        check_vma=False,
    )
```

profile of v0, /device:TPU:32, one launch (start us, length us, event | category | flops | bytes accessed | tf_op | source)
XLA Modules:
  0.0 507.5 jit_solution(15915799173783199281)
XLA Ops:
  7.3 0.7 copy-done
  7.9 0.4 compare_reduce_fusion
  8.4 0.1 broadcast_in_dim.15
  8.5 0.9 bitcast_select_fusion
  9.5 1.9 collective-permute-start
  11.4 1.3 collective-permute-done
  12.8 2.6 collective-permute-start.1
  15.4 7.6 %collective-permute-done.1 = bf16[128,1024]{1,0:T(8,128)(2,1)S(1)} collective-permute-done((bf16[128,1024]{1,0:T(8,128)(2,1)S(1)}, bf16[128,1024]{1,0:T(8,128)(2,1)S(1)}, u32[]{:S(2)}, u32[]{:S(2)}) %collective-permute-start.1) | collective-permute-done | bytes 262176 | tf_op jit(solution)/shard_map/ppermute | solution.py:13
  23.0 0.1 maximum_select_fusion.1
  23.2 2.7 collective-permute-start.2
  25.9 24.4 %collective-permute-done.2 = bf16[256,1024]{1,0:T(8,128)(2,1)S(1)} collective-permute-done((bf16[256,1024]{1,0:T(8,128)(2,1)S(1)}, bf16[256,1024]{1,0:T(8,128)(2,1)S(1)}, u32[]{:S(2)}, u32[]{:S(2)}) %collective-permute-start.2) | collective-permute-done | bytes 524320 | tf_op jit(solution)/shard_map/ppermute | solution.py:13
  50.3 0.5 maximum_select_fusion
  50.8 3.2 collective-permute-start.3
  54.0 47.8 %collective-permute-done.3 = bf16[512,1024]{1,0:T(8,128)(2,1)S(1)} collective-permute-done((bf16[512,1024]{1,0:T(8,128)(2,1)S(1)}, bf16[512,1024]{1,0:T(8,128)(2,1)S(1)}, u32[]{:S(2)}, u32[]{:S(2)}) %collective-permute-start.3) | collective-permute-done | bytes 1048608 | tf_op jit(solution)/shard_map/ppermute | solution.py:19
  101.9 2.9 fusion
  104.7 2.6 fusion.6
  107.4 219.6 %reduce-scatter.2.cloned.1.call-done = f32[32,1024]{1,0:T(8,128)} async-done(((f32[512,1024]{1,0:T(8,128)}), f32[32,1024]{1,0:T(8,128)}) %reduce-scatter.2.cloned.1.call-update) | async-done | bytes 131088 | tf_op jit(solution)/shard_map/reduce_scatter | solution.py:63
  327.0 1.5 subtract_convert_fusion
  328.6 84.4 %all-gather.2.cloned.1.call-done = bf16[512,1024]{1,0:T(8,128)(2,1)} async-done(((bf16[32,1024]{1,0:T(8,128)(2,1)}), bf16[512,1024]{1,0:T(8,128)(2,1)}) %all-gather.2.cloned.1.call-update) | async-done | bytes 1048592 | tf_op jit(solution)/shard_map/all_gather | solution.py:72
  413.0 4.9 convolution_bitcast_fusion
  417.9 0.2 select_convert_fusion
  418.1 2.5 collective-permute-start.4
  420.6 44.0 %collective-permute-done.4 = bf16[2,256,1024]{2,1,0:T(8,128)(2,1)S(1)} collective-permute-done((bf16[2,256,1024]{2,1,0:T(8,128)(2,1)S(1)}, bf16[2,256,1024]{2,1,0:T(8,128)(2,1)S(1)}, u32[]{:S(2)}, u32[]{:S(2)}) %collective-permute-start.4) | collective-permute-done | bytes 1048608 | tf_op jit(solution)/shard_map/ppermute | solution.py:13
  464.6 0.6 convert_add_fusion
  465.4 1.9 collective-permute-start.5
  467.3 13.8 %collective-permute-done.5 = bf16[2,128,1024]{2,1,0:T(8,128)(2,1)S(1)} collective-permute-done((bf16[2,128,1024]{2,1,0:T(8,128)(2,1)S(1)}, bf16[2,128,1024]{2,1,0:T(8,128)(2,1)S(1)}, u32[]{:S(2)}, u32[]{:S(2)}) %collective-permute-start.5) | collective-permute-done | bytes 524320 | tf_op jit(solution)/shard_map/ppermute | solution.py:13
  481.1 0.3 convert_add_fusion.1
  481.4 1.9 collective-permute-start.6
  483.3 1.5 collective-permute-done.6
  485.0 1.9 collective-permute-start.7
  486.9 13.0 %collective-permute-done.7 = bf16[64,1024]{1,0:T(8,128)(2,1)S(1)} collective-permute-done((bf16[64,1024]{1,0:T(8,128)(2,1)S(1)}, bf16[64,1024]{1,0:T(8,128)(2,1)S(1)}, u32[]{:S(2)}, u32[]{:S(2)}) %collective-permute-start.7) | collective-permute-done | bytes 131104 | tf_op jit(solution)/shard_map/ppermute | solution.py:19
  499.9 0.8 fusion.11
  (18 shorter events, 0.5 us)
Async XLA Ops:
  7.2 0.8 copy-start
  7.2 319.8 %reduce-scatter.2.cloned.1.call-start = ((), (), s32[]{:S(2)}) async-start(), calls=%async_computation.1 | async-start | bytes 2228224 | tf_op jit(solution)/shard_map/reduce_scatter | solution.py:63
  9.5 3.2 collective-permute-start
  12.8 10.3 %collective-permute-start.1 = (bf16[128,1024]{1,0:T(8,128)(2,1)S(1)}, bf16[128,1024]{1,0:T(8,128)(2,1)S(1)}, u32[]{:S(2)}, u32[]{:S(2)}) collective-permute-start(bf16[128,1024]{1,0:T(8,128)(2,1)S(1)} %maximum_select_fusion.2), channel_id=1, source_target_pairs={{0,32},{16,48},{32,0},{48,16},{64,96},{80,112},{96,64},{112,80},{1... | collective-permute-start | bytes 786440 | tf_op jit(solution)/shard_map/ppermute | solution.py:13
  23.2 27.1 %collective-permute-start.2 = (bf16[256,1024]{1,0:T(8,128)(2,1)S(1)}, bf16[256,1024]{1,0:T(8,128)(2,1)S(1)}, u32[]{:S(2)}, u32[]{:S(2)}) collective-permute-start(bf16[256,1024]{1,0:T(8,128)(2,1)S(1)} %maximum_select_fusion.1), channel_id=1, source_target_pairs={{0,64},{16,80},{32,96},{48,112},{64,0},{80,16},{96,32},{112,48},{1... | collective-permute-start | bytes 1572872 | tf_op jit(solution)/shard_map/ppermute | solution.py:13
  50.8 53.9 %copy-start.2 = (bf16[2,1024,1024]{2,1,0:T(8,128)(2,1)S(1)}, bf16[2,1024,1024]{2,1,0:T(8,128)(2,1)}, u32[]{:S(2)}) copy-start(bf16[2,1024,1024]{2,1,0:T(8,128)(2,1)} %param.6) | copy-start | bytes 12582916
  50.8 51.0 %collective-permute-start.3 = (bf16[512,1024]{1,0:T(8,128)(2,1)S(1)}, bf16[512,1024]{1,0:T(8,128)(2,1)S(1)}, u32[]{:S(2)}, u32[]{:S(2)}) collective-permute-start(bf16[512,1024]{1,0:T(8,128)(2,1)S(1)} %maximum_select_fusion), channel_id=1, source_target_pairs={{0,128},{16,144},{32,160},{48,176},{64,192},{80,208},{96,224},{112... | collective-permute-start | bytes 3145736 | tf_op jit(solution)/shard_map/ppermute | solution.py:19
  107.3 219.7 %copy-start.1 = (bf16[32,1024]{1,0:T(8,128)(2,1)S(1)}, bf16[32,1024]{1,0:T(8,128)(2,1)}, u32[]{:S(2)}) copy-start(bf16[32,1024]{1,0:T(8,128)(2,1)} %param.7) | copy-start | bytes 196612
  107.3 305.7 %all-gather.2.cloned.1.call-start = ((), (), s32[]{:S(2)}) async-start(), calls=%async_computation.2 | async-start | bytes 1114112 | tf_op jit(solution)/shard_map/all_gather | solution.py:72
  418.1 46.5 %collective-permute-start.4 = (bf16[2,256,1024]{2,1,0:T(8,128)(2,1)S(1)}, bf16[2,256,1024]{2,1,0:T(8,128)(2,1)S(1)}, u32[]{:S(2)}, u32[]{:S(2)}) collective-permute-start(bf16[2,256,1024]{2,1,0:T(8,128)(2,1)S(1)} %select_convert_fusion), channel_id=1, source_target_pairs={{0,64},{16,80},{32,96},{48,112},{64,0},{80,16},{96,32},{112,48},{1... | collective-permute-start | bytes 3145736 | tf_op jit(solution)/shard_map/ppermute | solution.py:13
  465.4 15.7 %collective-permute-start.5 = (bf16[2,128,1024]{2,1,0:T(8,128)(2,1)S(1)}, bf16[2,128,1024]{2,1,0:T(8,128)(2,1)S(1)}, u32[]{:S(2)}, u32[]{:S(2)}) collective-permute-start(bf16[2,128,1024]{2,1,0:T(8,128)(2,1)S(1)} %select_convert_fusion.1), channel_id=1, source_target_pairs={{0,32},{16,48},{32,0},{48,16},{64,96},{80,112},{96,64},{112,80},{1... | collective-permute-start | bytes 1572872 | tf_op jit(solution)/shard_map/ppermute | solution.py:13
  481.4 3.4 collective-permute-start.6
  485.0 14.9 %collective-permute-start.7 = (bf16[64,1024]{1,0:T(8,128)(2,1)S(1)}, bf16[64,1024]{1,0:T(8,128)(2,1)S(1)}, u32[]{:S(2)}, u32[]{:S(2)}) collective-permute-start(bf16[64,1024]{1,0:T(8,128)(2,1)S(1)} %fusion.12), channel_id=1, source_target_pairs={{128,0},{144,16},{160,32},{176,48},{192,64},{208,80},{224,96},{240... | collective-permute-start | bytes 393224 | tf_op jit(solution)/shard_map/ppermute | solution.py:19
Sparse Core Ops, SparseCore 0:
  107.5 219.5 reduce-scatter.1
  330.8 82.2 all-gather.1
where the time goes:
time: 508 us
  waiting for transfers between devices  458 us (90%)
  starting transfers between devices  18.8 us (4%)
  between operations  14.4 us (3%)
  matrix products  10.3 us (2%)
  other arithmetic  5.64 us (1%)
    reduce_scatter x1, waiting for transfers between devices, local(): lax.psum_scatter(summed + jnp.dot(prior_all, decoders[1], preferred_eleme...  220 us
    ppermute x6, waiting for transfers between devices, swapped(): return lax.ppermute(value, axis, pairs)  92.6 us
    all_gather x1, waiting for transfers between devices, local(): lax.all_gather(errors_here, 'feat', axis=0, tiled=True)  84.4 us
    ppermute x2, waiting for transfers between devices, passed_along(): lax.ppermute(value, axis, [(source, source + steps) for source in range(f...  60.8 us
    ppermute x6, starting transfers between devices, swapped(): return lax.ppermute(value, axis, pairs)  13.6 us
  transfers between devices with their start and end apart: 10, of which 10 were waited for; matrix products, arithmetic and copies ran while one was open for 0% of the time, Pallas kernels for 0%

commit v1 on v0

--- a/solution.py
+++ b/solution.py
@@ -69,7 +69,9 @@
     errors_here = (recon_rows - targets.astype(jnp.float32)).astype(jnp.bfloat16)
     grad_terms = jnp.einsum(
         "tc,kfc->ktf",
-        lax.all_gather(errors_here, "feat", axis=0, tiled=True),
+        jnp.concatenate(
+            lax.all_to_all(jnp.stack([errors_here] * lax.axis_size("feat")), "feat", 0, 0), axis=0
+        ),
         decoders,
         preferred_element_type=jnp.float32,
     )

time: 508 us -> 449 us (0.88)
  waiting for transfers between devices: 458 us -> 370 us
  blocking collectives: 0 us -> 30.1 us
    all_gather x1 -> x0, waiting for transfers between devices: 84.4 us -> none  [local(): lax.all_gather(errors_here, 'feat', axis=0, tiled=True)]
    all_to_all x0 -> x1, blocking collectives: none -> 30.1 us  [local(): lax.all_to_all(jnp.stack([errors_here] * lax.axis_size('feat')), 'feat',...]
  transfers between devices with their start and end apart: 10 -> 9, of which waited for: 10 -> 9; matrix products, arithmetic and copies ran while one was open for 0% -> 0% of each run, Pallas kernels for 0% -> 0%
where the time goes in v1:
time: 449 us
  waiting for transfers between devices  370 us (82%)
  blocking collectives  30.1 us (7%)
  starting transfers between devices  18.7 us (4%)
  between operations  14.4 us (3%)
  matrix products  10 us (2%)
  other arithmetic  5.01 us (1%)
    reduce_scatter x1, waiting for transfers between devices, local(): lax.psum_scatter(summed + jnp.dot(prior_all, decoders[1], preferred_eleme...  220 us
    ppermute x6, waiting for transfers between devices, swapped(): return lax.ppermute(value, axis, pairs)  89 us
    ppermute x2, waiting for transfers between devices, passed_along(): lax.ppermute(value, axis, [(source, source + steps) for source in range(f...  60.8 us
    all_to_all x1, blocking collectives, local(): lax.all_to_all(jnp.stack([errors_here] * lax.axis_size('feat')), 'feat',...  30.1 us
    ppermute x6, starting transfers between devices, swapped(): return lax.ppermute(value, axis, pairs)  13.6 us
  transfers between devices with their start and end apart: 9, of which 9 were waited for; matrix products, arithmetic and copies ran while one was open for 0% of the time, Pallas kernels for 0%

profile of v1, /device:TPU:32, one launch (start us, length us, event | category | flops | bytes accessed | tf_op | source)
XLA Modules:
  0.0 448.8 jit_solution(7968806507836289974)
XLA Ops:
  7.3 0.7 copy-done
  7.9 0.4 compare_reduce_fusion
  8.4 0.1 broadcast_in_dim.15
  8.5 0.9 bitcast_select_fusion
  9.5 1.9 collective-permute-start
  11.4 1.3 collective-permute-done
  12.8 2.6 collective-permute-start.1
  15.4 7.6 %collective-permute-done.1 = bf16[128,1024]{1,0:T(8,128)(2,1)S(1)} collective-permute-done((bf16[128,1024]{1,0:T(8,128)(2,1)S(1)}, bf16[128,1024]{1,0:T(8,128)(2,1)S(1)}, u32[]{:S(2)}, u32[]{:S(2)}) %collective-permute-start.1) | collective-permute-done | bytes 262176 | tf_op jit(solution)/shard_map/ppermute | solution.py:13
  23.0 0.1 maximum_select_fusion.1
  23.2 2.7 collective-permute-start.2
  25.9 24.4 %collective-permute-done.2 = bf16[256,1024]{1,0:T(8,128)(2,1)S(1)} collective-permute-done((bf16[256,1024]{1,0:T(8,128)(2,1)S(1)}, bf16[256,1024]{1,0:T(8,128)(2,1)S(1)}, u32[]{:S(2)}, u32[]{:S(2)}) %collective-permute-start.2) | collective-permute-done | bytes 524320 | tf_op jit(solution)/shard_map/ppermute | solution.py:13
  50.3 0.5 maximum_select_fusion
  50.8 3.2 collective-permute-start.3
  54.0 47.8 %collective-permute-done.3 = bf16[512,1024]{1,0:T(8,128)(2,1)S(1)} collective-permute-done((bf16[512,1024]{1,0:T(8,128)(2,1)S(1)}, bf16[512,1024]{1,0:T(8,128)(2,1)S(1)}, u32[]{:S(2)}, u32[]{:S(2)}) %collective-permute-start.3) | collective-permute-done | bytes 1048608 | tf_op jit(solution)/shard_map/ppermute | solution.py:19
  101.9 2.9 fusion
  104.7 2.6 fusion.6
  107.4 219.7 %reduce-scatter.2.cloned.1.call-done = f32[32,1024]{1,0:T(8,128)} async-done(((f32[512,1024]{1,0:T(8,128)}), f32[32,1024]{1,0:T(8,128)}) %reduce-scatter.2.cloned.1.call-update) | async-done | bytes 131088 | tf_op jit(solution)/shard_map/reduce_scatter | solution.py:63
  327.0 0.9 subtract_convert_fusion
  328.1 30.1 %all_to_all.5 = bf16[16,32,1024]{2,1,0:T(8,128)(2,1)S(1)} all-to-all(bf16[16,32,1024]{2,1,0:T(8,128)(2,1)S(1)} %stack.2), channel_id=1, replica_groups=mesh['layer'=32,'feat'=16] {'feat'}, dimensions={0} | all-to-all | bytes 2097152 | tf_op jit(solution)/shard_map/all_to_all | solution.py:73
  358.2 4.6 %convolution_bitcast_fusion = f32[2,512,1024]{2,1,0:T(8,128)S(1)} fusion(bf16[512,1024,1]{1,0,2:T(8,128)(2,1)S(1)} %bitcast.32, bf16[2,1024,1024]{2,1,0:T(8,128)(2,1)} %param.6), kind=kOutput, calls=%fused_computation | convolution fusion | flops 2147483648 | bytes 9437184 | tf_op jit(solution)/shard_map/tc,kfc->ktf/dot_general | solution.py:70
  362.7 0.2 select_convert_fusion
  362.9 2.5 collective-permute-start.4
  365.5 40.4 %collective-permute-done.4 = bf16[2,256,1024]{2,1,0:T(8,128)(2,1)S(1)} collective-permute-done((bf16[2,256,1024]{2,1,0:T(8,128)(2,1)S(1)}, bf16[2,256,1024]{2,1,0:T(8,128)(2,1)S(1)}, u32[]{:S(2)}, u32[]{:S(2)}) %collective-permute-start.4) | collective-permute-done | bytes 1048608 | tf_op jit(solution)/shard_map/ppermute | solution.py:13
  405.9 0.6 convert_add_fusion
  406.6 1.9 collective-permute-start.5
  408.5 13.8 %collective-permute-done.5 = bf16[2,128,1024]{2,1,0:T(8,128)(2,1)S(1)} collective-permute-done((bf16[2,128,1024]{2,1,0:T(8,128)(2,1)S(1)}, bf16[2,128,1024]{2,1,0:T(8,128)(2,1)S(1)}, u32[]{:S(2)}, u32[]{:S(2)}) %collective-permute-start.5) | collective-permute-done | bytes 524320 | tf_op jit(solution)/shard_map/ppermute | solution.py:13
  422.3 0.3 convert_add_fusion.1
  422.6 1.9 collective-permute-start.6
  424.6 1.5 collective-permute-done.6
  426.2 1.9 collective-permute-start.7
  428.1 13.0 %collective-permute-done.7 = bf16[64,1024]{1,0:T(8,128)(2,1)S(1)} collective-permute-done((bf16[64,1024]{1,0:T(8,128)(2,1)S(1)}, bf16[64,1024]{1,0:T(8,128)(2,1)S(1)}, u32[]{:S(2)}, u32[]{:S(2)}) %collective-permute-start.7) | collective-permute-done | bytes 131104 | tf_op jit(solution)/shard_map/ppermute | solution.py:19
  441.2 0.8 fusion.10
  (19 shorter events, 0.6 us)
Async XLA Ops:
  7.2 0.8 copy-start
  7.2 319.8 %reduce-scatter.2.cloned.1.call-start = ((), (), s32[]{:S(2)}) async-start(), calls=%async_computation.2 | async-start | bytes 2228224 | tf_op jit(solution)/shard_map/reduce_scatter | solution.py:63
  9.5 3.2 collective-permute-start
  12.8 10.3 %collective-permute-start.1 = (bf16[128,1024]{1,0:T(8,128)(2,1)S(1)}, bf16[128,1024]{1,0:T(8,128)(2,1)S(1)}, u32[]{:S(2)}, u32[]{:S(2)}) collective-permute-start(bf16[128,1024]{1,0:T(8,128)(2,1)S(1)} %maximum_select_fusion.2), channel_id=1, source_target_pairs={{0,32},{16,48},{32,0},{48,16},{64,96},{80,112},{96,64},{112,80},{1... | collective-permute-start | bytes 786440 | tf_op jit(solution)/shard_map/ppermute | solution.py:13
  23.2 27.1 %collective-permute-start.2 = (bf16[256,1024]{1,0:T(8,128)(2,1)S(1)}, bf16[256,1024]{1,0:T(8,128)(2,1)S(1)}, u32[]{:S(2)}, u32[]{:S(2)}) collective-permute-start(bf16[256,1024]{1,0:T(8,128)(2,1)S(1)} %maximum_select_fusion.1), channel_id=1, source_target_pairs={{0,64},{16,80},{32,96},{48,112},{64,0},{80,16},{96,32},{112,48},{1... | collective-permute-start | bytes 1572872 | tf_op jit(solution)/shard_map/ppermute | solution.py:13
  50.8 53.9 %copy-start.3 = (bf16[2,1024,1024]{2,1,0:T(8,128)(2,1)S(1)}, bf16[2,1024,1024]{2,1,0:T(8,128)(2,1)}, u32[]{:S(2)}) copy-start(bf16[2,1024,1024]{2,1,0:T(8,128)(2,1)} %param.6) | copy-start | bytes 12582916
  50.8 51.0 %collective-permute-start.3 = (bf16[512,1024]{1,0:T(8,128)(2,1)S(1)}, bf16[512,1024]{1,0:T(8,128)(2,1)S(1)}, u32[]{:S(2)}, u32[]{:S(2)}) collective-permute-start(bf16[512,1024]{1,0:T(8,128)(2,1)S(1)} %maximum_select_fusion), channel_id=1, source_target_pairs={{0,128},{16,144},{32,160},{48,176},{64,192},{80,208},{96,224},{112... | collective-permute-start | bytes 3145736 | tf_op jit(solution)/shard_map/ppermute | solution.py:19
  107.3 219.7 %copy-start.2 = (bf16[32,1024]{1,0:T(8,128)(2,1)S(1)}, bf16[32,1024]{1,0:T(8,128)(2,1)}, u32[]{:S(2)}) copy-start(bf16[32,1024]{1,0:T(8,128)(2,1)} %param.7) | copy-start | bytes 196612
  327.9 34.8 %copy-start.1 = (bf16[32,1024]{1,0:T(8,128)(2,1)}, bf16[32,1024]{1,0:T(8,128)(2,1)S(1)}, u32[]{:S(2)}) copy-start(bf16[32,1024]{1,0:T(8,128)(2,1)S(1)} %subtract_convert_fusion) | copy-start | bytes 196612
  362.9 42.9 %collective-permute-start.4 = (bf16[2,256,1024]{2,1,0:T(8,128)(2,1)S(1)}, bf16[2,256,1024]{2,1,0:T(8,128)(2,1)S(1)}, u32[]{:S(2)}, u32[]{:S(2)}) collective-permute-start(bf16[2,256,1024]{2,1,0:T(8,128)(2,1)S(1)} %select_convert_fusion), channel_id=1, source_target_pairs={{0,64},{16,80},{32,96},{48,112},{64,0},{80,16},{96,32},{112,48},{1... | collective-permute-start | bytes 3145736 | tf_op jit(solution)/shard_map/ppermute | solution.py:13
  406.6 15.7 %collective-permute-start.5 = (bf16[2,128,1024]{2,1,0:T(8,128)(2,1)S(1)}, bf16[2,128,1024]{2,1,0:T(8,128)(2,1)S(1)}, u32[]{:S(2)}, u32[]{:S(2)}) collective-permute-start(bf16[2,128,1024]{2,1,0:T(8,128)(2,1)S(1)} %select_convert_fusion.1), channel_id=1, source_target_pairs={{0,32},{16,48},{32,0},{48,16},{64,96},{80,112},{96,64},{112,80},{1... | collective-permute-start | bytes 1572872 | tf_op jit(solution)/shard_map/ppermute | solution.py:13
  422.6 3.4 collective-permute-start.6
  426.2 14.9 %collective-permute-start.7 = (bf16[64,1024]{1,0:T(8,128)(2,1)S(1)}, bf16[64,1024]{1,0:T(8,128)(2,1)S(1)}, u32[]{:S(2)}, u32[]{:S(2)}) collective-permute-start(bf16[64,1024]{1,0:T(8,128)(2,1)S(1)} %fusion.11), channel_id=1, source_target_pairs={{128,0},{144,16},{160,32},{176,48},{192,64},{208,80},{224,96},{240... | collective-permute-start | bytes 393224 | tf_op jit(solution)/shard_map/ppermute | solution.py:19
Sparse Core Ops, SparseCore 0:
  107.5 219.5 reduce-scatter.1
